TPU v7x, 256 devices: a whole 4x4x8 slice. The times are simulated.
256 devices in a mesh: grp: 16 (over y, z_hi, core), dev: 16 (over z_lo, x).
Axes of the slice: x: 4, y: 4, z: 8 (z_hi: 2, z_lo: 4; z = z_hi * 4 + z_lo), core: 2. Of those that a mesh axis runs over, the one named last changes fastest.
Arguments:
- panels: bfloat16 [256, 1536, 512], P(('grp', 'dev')), may hold values from -0.19921875 to 0.19921875
- panel_owner: int32 [16, 3], replicated, may hold values from 0 to 15, as said below
- interface_cols: bfloat16 [1536, 65536], P(None, ('grp', 'dev')), may hold values from -6 to 6
- border: bfloat16 [16384, 1536], P('grp', 'dev'), may hold values from -0.15625 to 0.15625
- block_rows: int32 [16, 8], replicated, may hold values from 0 to 31, as said below
- pattern: int32 [32, 32], P('grp', 'dev'), may hold values 0 or 1
- block_x: bfloat16 [4096, 256], P('dev'), may hold values from -0.09375 to 0.09375
Outputs:
- schur: bfloat16 [4096, 4096], P('grp', 'dev')
- product: float32 [4096, 256], P('grp')
Inputs may be any that keep to these rules, and one draw needn't show every extreme that they name: `panel_owner`: in each row the values are distinct. `block_rows`: in each row the values are distinct; for each subdomain the block rows with the same value of block // 2 (their owner group) come exactly 2 at a time; in every draw some owner group receives 2 block rows from every subdomain.
All inputs are finite; a program needn't handle non-finite values. No bound on the sum of `pattern` on one device may be relied on, other than what follows from the above.
Results may differ from a plain program's by a relative error of at most 0.017.
Values may be sent and summed in bfloat16 or wider, within the bound.
No kernel may reach another device: no remote copies, remote signals or barrier semaphores. Data moves between devices by JAX's collectives and lax.ppermute only.
A program may use at most 64 MiB of HBM per device.

v0:
```python
import jax
import jax.numpy as jnp
from jax import lax
from jax.sharding import PartitionSpec as P


def from_root(value, axis, source):
    kept = jnp.where(lax.axis_index(axis) == source, value, 0).astype(value.dtype)
    return lax.psum(kept, axis)


def local(panels, panel_owner, interface_cols, border, block_rows, pattern, block_x):
    group = lax.axis_index("grp")
    owners = lax.dynamic_slice_in_dim(panel_owner, group, 1, 0)[0]
    stored = panels[0]
    width = stored.shape[1]
    count_panels = stored.shape[0] // width
    columns = interface_cols.shape[1]
    lower = lax.broadcasted_iota(jnp.int32, (width, width), 0) > lax.broadcasted_iota(
        jnp.int32, (width, width), 1
    )
    unit = jnp.eye(width, dtype=jnp.bfloat16)
    remain = [
        interface_cols[step * width : (step + 1) * width].astype(jnp.float32)
        for step in range(count_panels)
    ]
    solved = []
    for step in range(count_panels):
        received = from_root(stored[step * width :], "dev", owners[step])
        inverse = jnp.where(lower, received[:width], jnp.zeros((), jnp.bfloat16)) + unit
        current = jnp.dot(
            inverse, remain[step].astype(jnp.bfloat16), preferred_element_type=jnp.float32
        ).astype(jnp.bfloat16)
        solved.append(current)
        if step + 1 < count_panels:
            below = jnp.dot(received[width:], current, preferred_element_type=jnp.float32)
            for later in range(step + 1, count_panels):
                offset = (later - step - 1) * width
                remain[later] = remain[later] - below[offset : offset + width]
    answer = jnp.concatenate(solved, axis=0)
    tile = jnp.dot(
        lax.all_gather(border, "dev", axis=1, tiled=True),
        answer,
        preferred_element_type=jnp.float32,
    )
    owned = pattern.shape[0]
    col_blocks = pattern.shape[1]
    block_size = columns // col_blocks
    per_group = block_rows.shape[1]
    tile_flat = tile.reshape(per_group, block_size * columns)
    my_list = lax.dynamic_slice_in_dim(block_rows, group, 1, 0)[0]
    targets = lax.broadcasted_iota(jnp.int32, (owned * lax.axis_size("grp"), 1), 0)
    onehot = (targets == my_list[None, :]).astype(jnp.float32)
    own_rows = lax.psum_scatter(
        jnp.dot(
            onehot, tile_flat, precision=lax.Precision.HIGHEST, preferred_element_type=jnp.float32
        ),
        "grp",
        scatter_dimension=0,
        tiled=True,
    )
    masked = (
        own_rows.reshape(owned, block_size, col_blocks, block_size)
        * pattern.astype(jnp.float32)[:, None, :, None]
    )
    schur = masked.reshape(owned * block_size, columns).astype(jnp.bfloat16)
    partial_sum = jnp.dot(schur, block_x, preferred_element_type=jnp.float32)
    product = lax.psum(partial_sum.astype(jnp.bfloat16), "dev").astype(jnp.float32)
    return (schur, product)


def solution(mesh):
    return jax.shard_map(
        local,
        mesh=mesh,
        in_specs=(
            P(("grp", "dev"), None, None),
            P(),
            P(None, ("grp", "dev")),
            P("grp", "dev"),
            P(),
            P("grp", "dev"),
            P("dev", None),
        ),
        out_specs=(P("grp", "dev"), P("grp", None)),
        check_vma=False,
    )
```

profile of v0, /device:TPU:8, one launch (start us, length us, event | category | flops | bytes accessed | tf_op | source)
XLA Modules:
  0.0 684.9 jit_solution(15940117969931973138)
XLA Ops:
  7.2 0.8 constant_dynamic-slice_fusion.1
  8.0 0.5 fusion.41
  9.8 1.3 select_bitcast_fusion
  11.1 0.7 copy-done.1
  11.8 1.1 select_bitcast_fusion.1
  13.5 0.9 select_bitcast_fusion.2
  14.5 0.7 all-gather.2.cloned.1.call-update
  15.4 175.8 %all-reduce.10.cloned.1.call-done = (bf16[1024,512]{1,0:T(8,128)(2,1)}, bf16[1536,512]{1,0:T(8,128)(2,1)}, bf16[512,512]{1,0:T(8,128)(2,1)}) async-done(((bf16[1024,512]{1,0:T(8,128)(2,1)}, bf16[1536,512]{1,0:T(8,128)(2,1)}, bf16[512,512]{1,0:T(8,128)(2,1)}), (bf16[1024,512]{1,0:T(8,128)(2,1)}, bf16[1536,512]{1,0:T(8,128)(2,1)}, bf16[512,512]{1,0:T(8,128)(2,1)})) %all-reduce.10.cloned.1.call-update) | async-done | bytes 3145744 | tf_op jit(solution)/shard_map/psum | solution.py:9
  191.2 1.5 convolution_convert_fusion.2
  192.8 0.4 fusion.1
  193.2 0.8 copy-done.6
  194.0 0.3 convolution_convert_fusion.1
  194.3 2.5 convolution_convert_fusion
  196.8 78.6 %all-gather.2.cloned.1.call-done = bf16[1024,1536]{0,1:T(8,128)(2,1)} async-done(((bf16[1024,96]{0,1:T(8,128)(2,1)}), bf16[1024,1536]{0,1:T(8,128)(2,1)}) %all-gather.2.cloned.1.call-update) | async-done | bytes 3145744 | tf_op jit(solution)/shard_map/all_gather | solution.py:42
  275.4 3.0 convolution_bitcast_fusion
  278.4 0.3 copy.10
  278.9 3.7 fusion.35
  282.7 0.6 copy-done.5
  283.4 0.6 dynamic-slice
  284.6 227.1 %all-reduce.8.cloned.1.call-done = f32[32,32768]{1,0:T(8,128)} async-done(((f32[32,32768]{1,0:T(8,128)}), f32[32,32768]{1,0:T(8,128)}) %all-reduce.8.cloned.1.call-update) | async-done | bytes 4194320
  511.7 1.3 constant_dynamic-slice_fusion
  513.5 0.8 convolution_convert_fusion.3
  514.4 162.4 %all-reduce.6.cloned.1.call-done = bf16[256,256]{1,0:T(8,128)(2,1)} async-done(((bf16[256,256]{1,0:T(8,128)(2,1)}), bf16[256,256]{1,0:T(8,128)(2,1)}) %all-reduce.6.cloned.1.call-update) | async-done | bytes 131088 | tf_op jit(solution)/shard_map/psum | solution.py:68
  676.7 1.6 convert_element_type.60
  (28 shorter events, 1.1 us)
Async XLA Ops:
  7.2 506.3 %copy-start = (bf16[256,256]{1,0:T(8,128)(2,1)S(1)}, bf16[256,256]{1,0:T(8,128)(2,1)}, u32[]{:S(2)}) copy-start(bf16[256,256]{1,0:T(8,128)(2,1)} %param.13) | copy-start | bytes 393220
  7.2 184.0 %all-reduce.10.cloned.1.call-start = ((), (), s32[]{:S(2)}) async-start(), calls=%async_computation.3 | async-start | bytes 6291456 | tf_op jit(solution)/shard_map/psum | solution.py:9
  9.8 2.0 copy-start.1
  14.4 0.8 copy-start.4
  14.4 176.8 %copy-start.7 = (bf16[1536,256]{1,0:T(8,128)(2,1)S(1)}, bf16[1536,256]{1,0:T(8,128)(2,1)}, u32[]{:S(2)}) copy-start(bf16[1536,256]{1,0:T(8,128)(2,1)} %param.9) | copy-start | bytes 2359300
  14.4 261.0 %all-gather.2.cloned.1.call-start = ((), (), s32[]{:S(2)}) async-start(), calls=%async_computation | async-start | bytes 3342336 | tf_op jit(solution)/shard_map/all_gather | solution.py:42
  15.2 496.5 %all-reduce.8.cloned.1.call-start = ((), (), s32[]{:S(2)}) async-start(), calls=%async_computation.2 | async-start | bytes 8388608
  191.2 1.6 copy-start.2
  192.8 1.2 copy-start.6
  282.7 0.7 copy-start.5
  282.7 0.7 copy-start.8
  282.7 394.0 %all-reduce.6.cloned.1.call-start = ((), (), s32[]{:S(2)}) async-start(), calls=%async_computation.1 | async-start | bytes 262144 | tf_op jit(solution)/shard_map/psum | solution.py:68
  513.5 164.9 %copy-start.3 = (bf16[256,256]{1,0:T(8,128)(2,1)}, bf16[256,256]{1,0:T(8,128)(2,1)S(1)}, u32[]{:S(2)}) copy-start(bf16[256,256]{1,0:T(8,128)(2,1)S(1)} %fusion.28) | copy-start | bytes 393220
Sparse Core Ops, SparseCore 0:
  14.6 176.6 all-reduce.9
  193.0 82.3 all-gather.1
  282.8 228.8 all-reduce.7
  514.8 161.9 all-reduce.5
where the time goes:
time: 685 us
  waiting for transfers between devices  645 us (94%)
  between operations  16.5 us (2%)
  matrix products  12.3 us (2%)
    unnamed x5, waiting for transfers between devices  228 us
    psum x1, waiting for transfers between devices, from_root(): return lax.psum(kept, axis)  176 us
    psum x1, waiting for transfers between devices, local(): lax.psum(partial_sum.astype(jnp.bfloat16), 'dev').astype(jnp.float32)  162 us
    all_gather x1, waiting for transfers between devices, local(): lax.all_gather(border, 'dev', axis=1, tiled=True)  78.6 us
  transfers between devices with their start and end apart: 4, of which 4 were waited for; matrix products, arithmetic and copies ran while one was open for 1% of the time, Pallas kernels for 0%

commit v1 on v0

--- a/solution.py
+++ b/solution.py
@@ -2,6 +2,11 @@
 import jax.numpy as jnp
 from jax import lax
 from jax.sharding import PartitionSpec as P
+
+
+def all_by_exchange(x, name, dim):
+    sent = jnp.stack([x] * lax.axis_size(name))
+    return jnp.concatenate(lax.all_to_all(sent, name, 0, 0), axis=dim)
 
 
 def from_root(value, axis, source):
@@ -38,11 +43,7 @@
                 offset = (later - step - 1) * width
                 remain[later] = remain[later] - below[offset : offset + width]
     answer = jnp.concatenate(solved, axis=0)
-    tile = jnp.dot(
-        lax.all_gather(border, "dev", axis=1, tiled=True),
-        answer,
-        preferred_element_type=jnp.float32,
-    )
+    tile = jnp.dot(all_by_exchange(border, "dev", 1), answer, preferred_element_type=jnp.float32)
     owned = pattern.shape[0]
     col_blocks = pattern.shape[1]
     block_size = columns // col_blocks

time: 685 us -> 631 us (0.921)
  waiting for transfers between devices: 645 us -> 579 us
  starting transfers between devices: 0.16 us -> 8.77 us
    all_gather x1 -> x0, waiting for transfers between devices: 78.6 us -> none  [local(): lax.all_gather(border, 'dev', axis=1, tiled=True)]
    psum x1, waiting for transfers between devices: 176 us -> 189 us  [from_root(): return lax.psum(kept, axis)]
    all_to_all x0 -> x1, starting transfers between devices: none -> 8.64 us  [all_by_exchange(): return jnp.concatenate(lax.all_to_all(sent, name, 0, 0), axis=dim)]
    unnamed x5 -> x4, waiting for transfers between devices: 228 us -> 227 us
  transfers between devices with their start and end apart: 4 -> 4, of which waited for: 4 -> 3; matrix products, arithmetic and copies ran while one was open for 1% -> 1% of each run, Pallas kernels for 0% -> 0%
where the time goes in v1:
time: 631 us; the launch traced here: 630 us
  waiting for transfers between devices  579 us (92%)
  between operations  16.5 us (3%)
  matrix products  12.3 us (2%)
  local copies, waits for them, and re-layouts  8.79 us (1%)
  starting transfers between devices  8.77 us (1%)
    unnamed x4, waiting for transfers between devices  227 us
    psum x1, waiting for transfers between devices, from_root(): return lax.psum(kept, axis)  189 us
    psum x1, waiting for transfers between devices, local(): lax.psum(partial_sum.astype(jnp.bfloat16), 'dev').astype(jnp.float32)  163 us
  transfers between devices with their start and end apart: 4, of which 3 were waited for; matrix products, arithmetic and copies ran while one was open for 1% of the time, Pallas kernels for 0%

profile of v1, /device:TPU:8, one launch (start us, length us, event | category | flops | bytes accessed | tf_op | source)
XLA Modules:
  0.0 630.4 jit_solution(4260850122319694274)
XLA Ops:
  7.2 3.0 stack.2
  10.2 8.6 %all-to-all-start = ((bf16[16,1024,96]{1,2,0:T(8,128)(2,1)}), bf16[16,1024,96]{1,2,0:T(8,128)(2,1)}, u32[]{:S(2)}, u32[]{:S(2)}) async-start(bf16[16,1024,96]{1,2,0:T(8,128)(2,1)} %stack.2), calls=%async_computation | async-start | bytes 6291456 | tf_op jit(solution)/shard_map/all_to_all | solution.py:9
  19.0 0.6 fusion.41
  21.5 0.8 select_bitcast_fusion.2
  22.4 1.1 select_bitcast_fusion.1
  23.5 1.3 select_bitcast_fusion
  24.9 0.6 copy-done.4
  25.7 189.5 %all-reduce.10.cloned.1.call-done = (bf16[1024,512]{1,0:T(8,128)(2,1)}, bf16[1536,512]{1,0:T(8,128)(2,1)}, bf16[512,512]{1,0:T(8,128)(2,1)}) async-done(((bf16[1024,512]{1,0:T(8,128)(2,1)}, bf16[1536,512]{1,0:T(8,128)(2,1)}, bf16[512,512]{1,0:T(8,128)(2,1)}), (bf16[1024,512]{1,0:T(8,128)(2,1)}, bf16[1536,512]{1,0:T(8,128)(2,1)}, bf16[512,512]{1,0:T(8,128)(2,1)})) %all-reduce.10.cloned.1.call-update) | async-done | bytes 3145744 | tf_op jit(solution)/shard_map/psum | solution.py:14
  215.1 1.5 convolution_convert_fusion.2
  216.7 0.4 fusion.1
  217.1 0.8 copy-done.7
  217.9 0.3 convolution_convert_fusion.1
  218.3 2.5 convolution_convert_fusion
  220.8 3.0 convolution_bitcast_fusion
  223.7 0.3 copy.11
  224.3 3.7 fusion.35
  228.1 0.6 copy-done.6
  228.7 0.6 dynamic-slice
  229.9 227.2 %all-reduce.8.cloned.1.call-done = f32[32,32768]{1,0:T(8,128)} async-done(((f32[32,32768]{1,0:T(8,128)}), f32[32,32768]{1,0:T(8,128)}) %all-reduce.8.cloned.1.call-update) | async-done | bytes 4194320
  457.1 1.3 constant_dynamic-slice_fusion
  458.4 0.2 reshape.42
  458.9 0.8 convolution_convert_fusion.3
  459.7 162.5 %all-reduce.6.cloned.1.call-done = bf16[256,256]{1,0:T(8,128)(2,1)} async-done(((bf16[256,256]{1,0:T(8,128)(2,1)}), bf16[256,256]{1,0:T(8,128)(2,1)}) %all-reduce.6.cloned.1.call-update) | async-done | bytes 131088 | tf_op jit(solution)/shard_map/psum | solution.py:69
  622.3 1.6 convert_element_type.60
  (30 shorter events, 0.9 us)
Async XLA Ops:
  7.2 451.7 %copy-start = (bf16[256,256]{1,0:T(8,128)(2,1)S(1)}, bf16[256,256]{1,0:T(8,128)(2,1)}, u32[]{:S(2)}) copy-start(bf16[256,256]{1,0:T(8,128)(2,1)} %param.13) | copy-start | bytes 393220
  10.2 8.7 %copy-start.5 = (s32[16,3]{0,1:T(4,128)S(1)}, s32[16,3]{0,1:T(4,128)}, u32[]{:S(2)}) copy-start(s32[16,3]{0,1:T(4,128)} %param.8) | copy-start | bytes 580
  10.2 11.3 %copy-start.1 = (bf16[1,1536,512]{2,1,0:T(8,128)(2,1)S(1)}, bf16[1,1536,512]{2,1,0:T(8,128)(2,1)}, u32[]{:S(2)}) copy-start(bf16[1,1536,512]{2,1,0:T(8,128)(2,1)} %param.7) | copy-start | bytes 4718596
  10.2 210.5 %all-to-all-start = ((bf16[16,1024,96]{1,2,0:T(8,128)(2,1)}), bf16[16,1024,96]{1,2,0:T(8,128)(2,1)}, u32[]{:S(2)}, u32[]{:S(2)}) async-start(bf16[16,1024,96]{1,2,0:T(8,128)(2,1)} %stack.2), calls=%async_computation | async-start | bytes 6291456 | tf_op jit(solution)/shard_map/all_to_all | solution.py:9
  18.9 196.3 %all-reduce.10.cloned.1.call-start = ((), (), s32[]{:S(2)}) async-start(), calls=%async_computation.3 | async-start | bytes 6291456 | tf_op jit(solution)/shard_map/psum | solution.py:14
  24.8 0.7 copy-start.4
  24.8 190.3 %copy-start.8 = (bf16[1536,256]{1,0:T(8,128)(2,1)S(1)}, bf16[1536,256]{1,0:T(8,128)(2,1)}, u32[]{:S(2)}) copy-start(bf16[1536,256]{1,0:T(8,128)(2,1)} %param.9) | copy-start | bytes 2359300
  24.8 432.3 %all-reduce.8.cloned.1.call-start = ((), (), s32[]{:S(2)}) async-start(), calls=%async_computation.2 | async-start | bytes 8388608
  215.1 1.6 copy-start.2
  216.7 1.2 copy-start.7
  228.0 0.7 copy-start.6
  228.0 0.7 copy-start.9
  228.0 394.2 %all-reduce.6.cloned.1.call-start = ((), (), s32[]{:S(2)}) async-start(), calls=%async_computation.1 | async-start | bytes 262144 | tf_op jit(solution)/shard_map/psum | solution.py:69
  458.9 165.0 %copy-start.3 = (bf16[256,256]{1,0:T(8,128)(2,1)}, bf16[256,256]{1,0:T(8,128)(2,1)S(1)}, u32[]{:S(2)}) copy-start(bf16[256,256]{1,0:T(8,128)(2,1)S(1)} %fusion.28) | copy-start | bytes 393220
Sparse Core Ops, SparseCore 0:
  24.9 190.1 all-reduce.9
  228.2 228.9 all-reduce.7
  460.3 161.9 all-reduce.5

commit v2 on v0

--- a/solution.py
+++ b/solution.py
@@ -2,6 +2,10 @@
 import jax.numpy as jnp
 from jax import lax
 from jax.sharding import PartitionSpec as P
+
+
+def _meet_strings(field, axis_name):
+    return jnp.sum(lax.all_gather(field, axis_name=axis_name), 0)
 
 
 def from_root(value, axis, source):
@@ -65,7 +69,7 @@
     )
     schur = masked.reshape(owned * block_size, columns).astype(jnp.bfloat16)
     partial_sum = jnp.dot(schur, block_x, preferred_element_type=jnp.float32)
-    product = lax.psum(partial_sum.astype(jnp.bfloat16), "dev").astype(jnp.float32)
+    product = _meet_strings(partial_sum.astype(jnp.bfloat16), "dev").astype(jnp.float32)
     return (schur, product)
 
 

time: 685 us -> 608 us (0.89)
  waiting for transfers between devices: 645 us -> 566 us
    psum x1 -> x0, waiting for transfers between devices: 162 us -> none  [local(): lax.psum(partial_sum.astype(jnp.bfloat16), 'dev').astype(jnp.float32)]
    all_gather x0 -> x1, waiting for transfers between devices: none -> 83.7 us  [_meet_strings(): return jnp.sum(lax.all_gather(field, axis_name=axis_name), 0)]
where the time goes in v2:
time: 608 us; the launch traced here: 607 us
  waiting for transfers between devices  566 us (93%)
  between operations  16.5 us (3%)
  matrix products  12.3 us (2%)
  local copies, waits for them, and re-layouts  6.48 us (1%)
    unnamed x5, waiting for transfers between devices  228 us
    psum x1, waiting for transfers between devices, from_root(): return lax.psum(kept, axis)  176 us
    all_gather x1, waiting for transfers between devices, _meet_strings(): return jnp.sum(lax.all_gather(field, axis_name=axis_name), 0)  83.7 us
    all_gather x1, waiting for transfers between devices, local(): lax.all_gather(border, 'dev', axis=1, tiled=True)  78.6 us
  transfers between devices with their start and end apart: 4, of which 4 were waited for; matrix products, arithmetic and copies ran while one was open for 1% of the time, Pallas kernels for 0%

profile of v2, /device:TPU:8, one launch (start us, length us, event | category | flops | bytes accessed | tf_op | source)
XLA Modules:
  0.0 607.2 jit_solution(14746926716882516615)
XLA Ops:
  7.2 0.8 constant_dynamic-slice_fusion.1
  8.0 0.5 fusion.41
  9.8 1.3 select_bitcast_fusion
  11.1 0.7 copy-done.1
  11.8 1.1 select_bitcast_fusion.1
  13.5 0.9 select_bitcast_fusion.2
  14.5 0.7 all-gather.4.cloned.1.call-update
  15.4 175.8 %all-reduce.7.cloned.1.call-done = (bf16[1024,512]{1,0:T(8,128)(2,1)}, bf16[1536,512]{1,0:T(8,128)(2,1)}, bf16[512,512]{1,0:T(8,128)(2,1)}) async-done(((bf16[1024,512]{1,0:T(8,128)(2,1)}, bf16[1536,512]{1,0:T(8,128)(2,1)}, bf16[512,512]{1,0:T(8,128)(2,1)}), (bf16[1024,512]{1,0:T(8,128)(2,1)}, bf16[1536,512]{1,0:T(8,128)(2,1)}, bf16[512,512]{1,0:T(8,128)(2,1)})) %all-reduce.7.cloned.1.call-update) | async-done | bytes 3145744 | tf_op jit(solution)/shard_map/psum | solution.py:13
  191.2 1.5 convolution_convert_fusion.2
  192.8 0.4 fusion.1
  193.2 0.8 copy-done.6
  194.0 0.3 convolution_convert_fusion.1
  194.3 2.5 convolution_convert_fusion
  196.8 78.6 %all-gather.4.cloned.1.call-done = bf16[1024,1536]{0,1:T(8,128)(2,1)} async-done(((bf16[1024,96]{0,1:T(8,128)(2,1)}), bf16[1024,1536]{0,1:T(8,128)(2,1)}) %all-gather.4.cloned.1.call-update) | async-done | bytes 3145744 | tf_op jit(solution)/shard_map/all_gather | solution.py:46
  275.4 3.0 convolution_bitcast_fusion
  278.9 3.7 fusion.35
  282.7 0.6 copy-done.5
  283.4 0.6 dynamic-slice
  284.6 227.1 %all-reduce.5.cloned.1.call-done = f32[32,32768]{1,0:T(8,128)} async-done(((f32[32,32768]{1,0:T(8,128)}), f32[32,32768]{1,0:T(8,128)}) %all-reduce.5.cloned.1.call-update) | async-done | bytes 4194320
  511.7 1.3 constant_dynamic-slice_fusion
  513.5 0.8 convolution_convert_fusion.3
  514.4 83.7 %all-gather.6.cloned.1.call-done = bf16[4096,256]{1,0:T(8,128)(2,1)} async-done(((bf16[256,256]{1,0:T(8,128)(2,1)}), bf16[4096,256]{1,0:T(8,128)(2,1)}) %all-gather.6.cloned.1.call-update) | async-done | bytes 2097168 | tf_op jit(solution)/shard_map/all_gather | solution.py:8
  598.0 1.9 reduce_sum.12
  599.9 0.7 convert_element_type.62
  (29 shorter events, 1.5 us)
Async XLA Ops:
  7.2 506.3 %copy-start = (bf16[256,256]{1,0:T(8,128)(2,1)S(1)}, bf16[256,256]{1,0:T(8,128)(2,1)}, u32[]{:S(2)}) copy-start(bf16[256,256]{1,0:T(8,128)(2,1)} %param.13) | copy-start | bytes 393220
  7.2 184.0 %all-reduce.7.cloned.1.call-start = ((), (), s32[]{:S(2)}) async-start(), calls=%async_computation.3 | async-start | bytes 6291456 | tf_op jit(solution)/shard_map/psum | solution.py:13
  9.8 2.0 copy-start.1
  14.4 0.8 copy-start.4
  14.4 176.8 %copy-start.7 = (bf16[1536,256]{1,0:T(8,128)(2,1)S(1)}, bf16[1536,256]{1,0:T(8,128)(2,1)}, u32[]{:S(2)}) copy-start(bf16[1536,256]{1,0:T(8,128)(2,1)} %param.9) | copy-start | bytes 2359300
  14.4 261.0 %all-gather.4.cloned.1.call-start = ((), (), s32[]{:S(2)}) async-start(), calls=%async_computation | async-start | bytes 3342336 | tf_op jit(solution)/shard_map/all_gather | solution.py:46
  15.2 496.5 %all-reduce.5.cloned.1.call-start = ((), (), s32[]{:S(2)}) async-start(), calls=%async_computation.2 | async-start | bytes 8388608
  191.2 1.6 copy-start.2
  192.8 1.2 copy-start.6
  282.7 0.7 copy-start.5
  282.7 0.7 copy-start.8
  282.7 315.3 %all-gather.6.cloned.1.call-start = ((), (), s32[]{:S(2)}) async-start(), calls=%async_computation.1 | async-start | bytes 2228224 | tf_op jit(solution)/shard_map/all_gather | solution.py:8
  513.5 87.2 %copy-start.3 = (bf16[256,256]{1,0:T(8,128)(2,1)}, bf16[256,256]{1,0:T(8,128)(2,1)S(1)}, u32[]{:S(2)}) copy-start(bf16[256,256]{1,0:T(8,128)(2,1)S(1)} %fusion.28) | copy-start | bytes 393220
Sparse Core Ops, SparseCore 0:
  14.6 176.6 all-reduce.6
  193.0 82.3 all-gather.3
  282.8 228.8 all-reduce.4
  514.5 83.5 all-gather.5
